TPU v7x, 256 devices: a whole 4x4x8 slice. The times are simulated.
256 devices in a mesh: tm: 64 (over x, y_hi, z), chan: 4 (over y_lo, core).
Axes of the slice: x: 4, y: 4 (y_hi: 2, y_lo: 2; y = y_hi * 2 + y_lo), z: 8, core: 2. Of those that a mesh axis runs over, the one named last changes fastest.
Arguments:
- features: bfloat16 [131072, 1024], P('tm', 'chan'), may hold values from -18 to 18
- rec_start: int32 [131072], P('tm'), may hold values from 0 to 131071, as said below
- rec_end: int32 [131072], P('tm'), may hold values from 1 to 131072, as said below
- w_value: bfloat16 [1024, 1024], P(None, 'chan'), may hold values from -0.1875 to 0.1875
- w_gate: bfloat16 [1024, 1024], P(None, 'chan'), may hold values from -0.1875 to 0.1875
- depth_kernel: bfloat16 [9, 1024], P(None, 'chan'), may hold values from -2 to 2
- norm_gain: bfloat16 [1024], P('chan'), may hold values from 0.099609375 to 1.8984375
- norm_shift: bfloat16 [1024], P('chan'), may hold values from -3 to 3
- w_down: bfloat16 [1024, 1024], P('chan'), may hold values from -0.1875 to 0.1875
Outputs:
- mixed: bfloat16 [131072, 1024], P('tm', 'chan')
Inputs may be any that keep to these rules, and one draw needn't show every extreme that they name: Frames are packed recordings in order: rec_start[t] <= t < rec_end[t], all frames of a recording share both values, and a recording ends where the next starts. Frame 0 is a recording of its own, and so is the last frame. `rec_end`: as for rec_start.
All inputs are finite; a program needn't handle non-finite values.
Results may differ from a plain program's by a relative error of at most 0.012.
Values may be sent and summed in bfloat16 or wider, within the bound.
No kernel may reach another device: no remote copies, remote signals or barrier semaphores. Data moves between devices by JAX's collectives and lax.ppermute only.
A program may use at most 64 MiB of HBM per device.

v0:
```python
import functools

import jax
import jax.numpy as jnp
from jax import lax
from jax.experimental import pallas as pl
from jax.experimental.pallas import tpu as pltpu
from jax.sharding import PartitionSpec as P


AXES = ("tm", "chan")
F32, BF16 = jnp.float32, jnp.bfloat16
LANES = 128
TAIL = 32


def permute(value, move):
    tms, chans = lax.axis_size("tm"), lax.axis_size("chan")
    pairs = []
    for t in range(tms):
        for c in range(chans):
            to_t, to_c = move(t, c)
            if 0 <= to_t < tms:
                pairs.append((t * chans + c, to_t * chans + to_c))
    return lax.ppermute(value, AXES, pairs)


def over_link(t, c):
    return t, c ^ 2


def over_other_link(t, c):
    return t ^ 8, c ^ 2


def to_core(t, c):
    return t, c ^ 1


def to_diagonal(t, c):
    return t, c ^ 3


def near(value):
    return pltpu.with_memory_space_constraint(value, pltpu.VMEM)


STEP = 16


def stage_kernel(stage, taps_count, rows, edge, *refs):
    refs = list(refs)
    own, mate, linked, far = [refs.pop(0) for _ in range(4)]
    halos = [refs.pop(0) for _ in range(4)] if stage == 3 else None
    weights = [refs.pop(0) for _ in range(2)]
    taps, start, end = [refs.pop(0) for _ in range(3)]
    tail = refs.pop(0) if stage > 0 else None
    head = refs.pop(0) if stage == 3 else None
    earlier = [refs.pop(0) for _ in range(3)] if stage == 3 else None
    conv_out, stats_out = refs.pop(0), refs.pop(0)
    tail_out = refs.pop(0) if stage < 3 else None
    head_out = refs.pop(0) if stage == 0 else None
    sent_out = refs.pop(0) if stage == 3 else None
    glu, conv = refs

    fresh = linked.shape[0]
    width = weights[0].shape[1]
    blocks = width // LANES
    half = taps_count // 2
    position = lax.axis_index("tm")

    def columns(j):
        return slice(j * LANES, (j + 1) * LANES)

    def put(row, value):
        for j in range(blocks):
            glu[j, row : row + value.shape[0], :] = value[:, columns(j)].astype(F32)

    def gated_of(parts):
        x = jnp.concatenate(parts, axis=1)
        value, gate = [jnp.dot(x, w[...], preferred_element_type=F32) for w in weights]
        return (value * (0.5 + 0.5 * jnp.tanh(0.5 * gate))).astype(BF16)

    if tail is not None:
        put(0, tail[...])
    for row in range(0, fresh, 256):
        at = stage * fresh + row
        parts = [own[at : at + 256, :], mate[at : at + 256, :], linked[row : row + 256, :], far[row : row + 256, :]]
        if halos is not None and row + 256 == fresh:
            parts = [jnp.concatenate([part, halo[...]], axis=0) for part, halo in zip(parts, halos)]
        gated = gated_of(parts)
        put(TAIL + row, gated)
        if head_out is not None and row == 0:
            head_out[...] = gated[:TAIL]
        if tail_out is not None and row + 256 == fresh:
            tail_out[...] = gated[256 - TAIL :]
    if stage == 3:
        put(TAIL + fresh + 16, head[...])

    total_rows = conv_out.shape[0]
    first = TAIL + 16 if stage == 0 else 16
    scale = [[jnp.broadcast_to(taps[k : k + 1, columns(j)], (8, LANES)) for k in range(taps_count)] for j in range(blocks)]
    line = lax.broadcasted_iota(jnp.int32, (STEP, LANES), 0) + position * rows

    def conv_rows(source, target, row, sums):
        frame = line + row
        lo, hi = start[pl.ds(target, STEP), :] - frame, end[pl.ds(target, STEP), :] - frame
        out = []
        for j in range(blocks):
            acc = None
            for k in range(taps_count):
                shift = k - half
                term = glu[j, pl.ds(source + shift, STEP), :]
                term = (term.reshape(STEP // 8, 8, LANES) * scale[j][k][None]).reshape(STEP, LANES)
                if shift < 0:
                    term = jnp.where(lo <= shift, term, 0.0)
                if shift > 0:
                    term = jnp.where(hi > shift, term, 0.0)
                acc = term if acc is None else acc + term
            conv[j, pl.ds(target, STEP), :] = acc
            out.append(sums[j] + jnp.sum(acc.reshape(STEP // 8, 8, LANES), axis=0))
        return tuple(out)

    zero = tuple(jnp.zeros((8, LANES), F32) for _ in range(blocks))
    straight = total_rows - 16 if stage == 3 else total_rows

    def step(i, sums):
        target = pl.multiple_of(i * STEP, STEP)
        return conv_rows(target + first, target, target + edge, sums)

    sums = lax.fori_loop(0, straight // STEP, step, zero, unroll=UNROLL)
    if stage == 3:
        sums = conv_rows(TAIL + fresh + 16, straight, 0, sums)

    means = [jnp.sum(s, axis=0, keepdims=True) * (1.0 / total_rows) for s in sums]
    means8 = [jnp.broadcast_to(m, (8, LANES)) for m in means]

    def centre(i, squares):
        target = pl.multiple_of(i * STEP, STEP)
        out = []
        for j in range(blocks):
            c = conv[j, pl.ds(target, STEP), :].reshape(STEP // 8, 8, LANES) - means8[j][None]
            conv_out[pl.ds(target, STEP), columns(j)] = c.reshape(STEP, LANES).astype(BF16)
            out.append(squares[j] + jnp.sum(c * c, axis=0))
        return tuple(out)

    squares = lax.fori_loop(0, total_rows // STEP, centre, zero, unroll=UNROLL)
    squares = [jnp.sum(q, axis=0, keepdims=True) for q in squares]
    count = jnp.full((1, LANES), float(total_rows), F32)
    if stage < 3:
        for j in range(blocks):
            stats_out[0:1, columns(j)] = means[j]
            stats_out[1:2, columns(j)] = squares[j]
            stats_out[2:3, columns(j)] = count
    else:
        for j in range(blocks):
            for k in range(3):
                stats_out[k : k + 1, columns(j)] = earlier[k][0:1, columns(j)]
            stats_out[3:4, columns(j)] = means[j]
    if sent_out is not None:
        totals = []
        for j in range(blocks):
            parts = [(ref[2:3, columns(j)], ref[0:1, columns(j)], ref[1:2, columns(j)]) for ref in earlier]
            parts.append((count, means[j], squares[j]))
            mean = sum(n * m for n, m, _ in parts) * (1.0 / rows)
            totals.append((mean, sum(q + n * (m - mean) * (m - mean) for n, m, q in parts)))
        piece = jnp.concatenate([t[0] for t in totals] + [t[1] for t in totals], axis=0)
        for i in range(sent_out.shape[0]):
            sent_out[i] = piece


UNROLL = 4


def stage_call(stage, taps_count, rows, edge, devices, xs, halos, weights, taps, start, end, tail, head, earlier):
    fresh, width = xs[2].shape[0], weights[0].shape[1]
    count = start.shape[0]
    margin = pltpu.VMEM((TAIL, width), BF16)
    outs = [pltpu.HBM((count, width), BF16), pltpu.VMEM((8, width), F32)]
    operands = list(xs)
    if stage == 3:
        operands += halos
    operands += [*weights, taps, start, end]
    if stage > 0:
        operands.append(tail)
    if stage == 3:
        operands += [head, *earlier]
    if stage < 3:
        outs.append(margin)
    if stage == 0:
        outs.append(margin)
    if stage == 3:
        outs.append(pltpu.VMEM((devices, 2 * width // LANES, LANES), F32))
    vmem = pl.BlockSpec(memory_space=pltpu.VMEM)
    return pl.pallas_call(
        functools.partial(stage_kernel, stage, taps_count, rows, edge),
        out_shape=outs,
        in_specs=[vmem] * len(operands),
        out_specs=[vmem] * len(outs),
        scratch_shapes=[
            pltpu.VMEM((width // LANES, TAIL + fresh + 16 + TAIL, LANES), F32),
            pltpu.VMEM((width // LANES, count, LANES), F32),
        ],
        cost_estimate=pl.CostEstimate(
            flops=16 * fresh * width * width, transcendentals=fresh * width, bytes_accessed=4 << 20
        ),
        compiler_params=pltpu.CompilerParams(vmem_limit_bytes=12 << 20),
    )(*[near(o) for o in operands])


def lay_out_kernel(value, gate, own_value, own_gate):
    depth = value.shape[0] // 4
    chan = lax.axis_index("chan")
    for i in range(4):
        rows = pl.ds(pl.multiple_of((chan ^ i) * depth, depth), depth)
        own_value[i * depth : (i + 1) * depth, :] = value[rows, :]
        own_gate[i * depth : (i + 1) * depth, :] = gate[rows, :]


def columns_kernel(down, *outs):
    width = down.shape[1] // 4
    chan = lax.axis_index("chan")
    for i in range(4):
        outs[i][...] = down[:, pl.ds(pl.multiple_of((chan ^ i) * width, width), width)]


def combine_kernel(rows, total, got, gain, shift, out):
    half = gain.shape[0]
    means = got[:, 0:half, :]
    mean = jnp.sum(means, axis=0) * (1.0 / got.shape[0])
    var = jnp.sum(got[:, half:, :] + rows * (means - mean) ** 2, axis=0) * (1.0 / total)
    scale = gain[...] / jnp.sqrt(var + 1e-05)
    out[0:half, :] = scale
    out[half:, :] = shift[...] - mean * scale


def hold_kernel(*refs):
    count = (len(refs) - 2) // 2
    sems = refs[-1]
    copies = [pltpu.make_async_copy(refs[i], refs[count + 1 + i], sems.at[i]) for i in range(count)]
    for copy in copies:
        copy.start()
    for copy in copies:
        copy.wait()


def finish_kernel(pieces, bounds, *refs):
    held, refs = refs[: 4 * pieces], refs[4 * pieces :]
    means, scales, weights, out = refs[:4], refs[4:8], refs[8:12], refs[12]
    width = out.shape[1]
    for piece in range(pieces):
        parts = []
        for block in range(4):
            for j in range(width // LANES):
                cut = slice(j * LANES, (j + 1) * LANES)
                a = scales[block][j : j + 1, :] * 0.5
                b = scales[block][width // LANES + j : width // LANES + j + 1, :] * 0.5
                b = b + means[block][piece : piece + 1, cut] * a
                h = held[block * pieces + piece][:, cut].astype(F32) * a + b
                parts.append((h + h * jnp.tanh(h)).astype(BF16))
        swished = jnp.concatenate(parts, axis=1)
        down = jnp.concatenate([w[...] for w in weights], axis=0)
        result = jnp.dot(swished, down, preferred_element_type=F32).astype(BF16)
        at = 0
        for first, size in bounds[piece]:
            out[first : first + size, :] = result[at : at + size]
            at += size


def body(
    features, rec_start, rec_end, w_value, w_gate, depth_kernel, norm_gain, norm_shift, w_down
):
    rows, width = features.shape
    taps_count = depth_kernel.shape[0]
    tms = lax.axis_size("tm")
    total = rows * tms
    chunk = rows // 4
    vmem = pl.BlockSpec(memory_space=pltpu.VMEM)

    first_chunk = features[:chunk]
    rest, _ = lax.optimization_barrier((features, first_chunk))
    linked = [permute(first_chunk, over_link)]
    for k in range(1, 4):
        linked.append(permute(rest[k * chunk : (k + 1) * chunk], over_link))

    weights = pl.pallas_call(
        lay_out_kernel,
        out_shape=[pltpu.VMEM(w_value.shape, BF16)] * 2,
        in_specs=[vmem] * 2,
        out_specs=[vmem] * 2,
        compiler_params=pltpu.CompilerParams(vmem_limit_bytes=8 << 20),
        name="lay_out",
    )(w_value, w_gate)

    halo = jnp.concatenate(
        [
            permute(rest[:8], lambda t, c: (t - 1, c)),
            permute(rest[rows - 8 :], lambda t, c: (t + 1, c)),
        ],
        axis=0,
    )
    halo_linked = permute(halo, over_link)
    halo_mate = permute(halo, to_core)
    halos = [halo, halo_mate, halo_linked, permute(halo_linked, to_core)]

    mate = permute(features, to_core)
    far = []
    for k in range(4):
        far.append(permute(linked[k], to_core))

    taps = jnp.pad(depth_kernel.astype(F32), ((0, 16 - taps_count), (0, 0)))

    downs = pl.pallas_call(
        columns_kernel,
        out_shape=[pltpu.HBM((width, width), BF16)] * 4,
        in_specs=[vmem],
        out_specs=[vmem] * 4,
        compiler_params=pltpu.CompilerParams(vmem_limit_bytes=4 << 20),
        name="columns",
    )(w_down)
    down = [downs[0]]
    for i, move in ((2, over_other_link), (1, to_core), (3, lambda t, c: (t ^ 8, c ^ 3))):
        down.append(permute(downs[i], move))

    edges = [16, chunk - 16, 2 * chunk - 16, 3 * chunk - 16, rows]

    def spread(vector, k):
        part = vector[edges[k] : edges[k + 1]]
        if k == 3:
            part = jnp.concatenate([part, vector[:16]])
        return jnp.broadcast_to(part[:, None], (part.shape[0], LANES))

    starts, ends = [spread(rec_start, k) for k in range(4)], [spread(rec_end, k) for k in range(4)]

    convs, stats, tail, head = [], [], None, None
    for k in range(4):
        if k == 2:
            tail, starts[3], ends[3] = lax.optimization_barrier((tail, starts[3], ends[3]))
        out = stage_call(
            k, taps_count, rows, edges[k], tms, [features, mate, linked[k], far[k]], halos, weights, taps,
            starts[k], ends[k], tail, head, stats,
        )
        convs.append(out[0])
        stats.append(out[1])
        tail = out[2] if k < 3 else None
        head = out[3] if k == 0 else head
    sent = out[2]

    def spread_out(k):
        over = permute(convs[k], over_link)
        mine = permute(convs[k], to_core)
        return convs[k], over, mine, permute(over, to_core)

    pieces = [spread_out(k) for k in range(4)]
    convs = [pieces[k][block] for block in range(4) for k in range(4)]
    means = [stats[3]]
    for move in (over_link, to_core, to_diagonal):
        means.append(permute(stats[3], move))

    got = lax.all_to_all(sent, "tm", 0, 0)
    half = width // LANES
    own_scale = pl.pallas_call(
        functools.partial(combine_kernel, float(rows), float(total)),
        out_shape=pltpu.VMEM((2 * half, LANES), F32),
        in_specs=[vmem] * 3,
        out_specs=vmem,
        compiler_params=pltpu.CompilerParams(vmem_limit_bytes=4 << 20),
        name="combine",
    )(near(got), near(norm_gain.astype(F32).reshape(half, LANES)), near(norm_shift.astype(F32).reshape(half, LANES)))
    scales = [own_scale]
    for move in (over_link, to_core, to_diagonal):
        scales.append(permute(own_scale, move))

    held = [*convs, *down]
    held = pl.pallas_call(
        hold_kernel,
        out_shape=[pltpu.VMEM(c.shape, c.dtype) for c in held],
        in_specs=[pl.BlockSpec(memory_space=pl.ANY)] * len(held) + [vmem],
        out_specs=[vmem] * len(held),
        scratch_shapes=[pltpu.SemaphoreType.DMA((len(held),))],
        compiler_params=pltpu.CompilerParams(vmem_limit_bytes=4 << 20),
        name="hold",
    )(*held, own_scale)
    convs, down = held[: len(convs)], held[len(convs) :]

    bounds = [[(edges[k], edges[k + 1] - edges[k])] for k in range(4)]
    bounds[3].append((0, 16))
    operands = [near(o) for o in [*convs, *means, *scales, *down]]
    return pl.pallas_call(
        functools.partial(finish_kernel, 4, bounds),
        out_shape=jax.ShapeDtypeStruct((rows, width), BF16),
        in_specs=[vmem] * len(operands),
        out_specs=vmem,
        cost_estimate=pl.CostEstimate(
            flops=8 * rows * width * width, transcendentals=rows * 4 * width, bytes_accessed=6 << 20
        ),
        compiler_params=pltpu.CompilerParams(vmem_limit_bytes=16 << 20),
        name="finish",
    )(*operands)


def solution(mesh):
    in_specs = (
        P("tm", "chan"),
        P("tm"),
        P("tm"),
        P(None, "chan"),
        P(None, "chan"),
        P(None, "chan"),
        P("chan"),
        P("chan"),
        P("chan", None),
    )
    out_specs = P("tm", "chan")

    return jax.shard_map(body, mesh=mesh, in_specs=in_specs, out_specs=out_specs, check_vma=False)
```

profile of v0, /device:TPU:1, one launch (start us, length us, event | category | flops | bytes accessed | tf_op | source)
XLA Modules:
  0.0 109.0 jit_solution(349427975615325576)
XLA Ops:
  0.0 3.2 %collective-permute-start = (bf16[2048,256]{1,0:T(8,128)(2,1)}, bf16[2048,256]{1,0:T(8,128)(2,1)S(1)}, u32[]{:S(2)}, u32[]{:S(2)}) collective-permute-start(bf16[2048,256]{1,0:T(8,128)(2,1)} %refs_0_.7), channel_id=1, source_target_pairs={{0,1},{1,0},{2,3},{3,2},{4,5},{5,4},{6,7},{7,6},{8,9},{9,8},{10,11... | collective-permute-start | bytes 3145736 | tf_op jit(solution)/shard_map/ppermute | solution.py:25
  7.7 1.5 %collective-permute-start.3 = (bf16[512,256]{1,0:T(8,128)(2,1)S(1)}, bf16[512,256]{1,0:T(8,128)(2,1)S(1)}, u32[]{:S(2)}, u32[]{:S(2)}) collective-permute-start(bf16[512,256]{1,0:T(8,128)(2,1)S(1)} %get-tuple-element.95), channel_id=1, source_target_pairs={{0,2},{1,3},{2,0},{3,1},{4,6},{5,7},{6,4},{7,5},{8,10},{9,11},{10,... | collective-permute-start | bytes 786440 | tf_op jit(solution)/shard_map/ppermute | solution.py:25
  9.8 3.6 %collective-permute-start.10 = (bf16[8,256]{1,0:T(8,128)(2,1)S(1)}, bf16[8,256]{1,0:T(8,128)(2,1)S(1)}, u32[]{:S(2)}, u32[]{:S(2)}) collective-permute-start(bf16[8,256]{1,0:T(8,128)(2,1)S(1)} %get-tuple-element.91), channel_id=1, source_target_pairs={{0,4},{1,5},{2,6},{3,7},{4,8},{5,9},{6,10},{7,11},{8,12},{9,13},{1... | collective-permute-start | bytes 12296 | tf_op jit(solution)/shard_map/ppermute | solution.py:25
  15.5 8.0 %collective-permute-done.12.refs_6_ = bf16[16,256]{1,0:T(8,128)(2,1)S(1)} collective-permute-done((bf16[16,256]{1,0:T(8,128)(2,1)S(1)}, bf16[16,256]{1,0:T(8,128)(2,1)S(1)}, u32[]{:S(2)}, u32[]{:S(2)}) %collective-permute-start.12) | collective-permute-done | bytes 8224 | tf_op jit(solution)/shard_map/ppermute | solution.py:25
  25.6 5.0 %collective-permute-done.7.refs_2_ = bf16[512,256]{1,0:T(8,128)(2,1)S(1)} collective-permute-done((bf16[512,256]{1,0:T(8,128)(2,1)S(1)}, bf16[512,256]{1,0:T(8,128)(2,1)S(1)}, u32[]{:S(2)}, u32[]{:S(2)}) %collective-permute-start.7) | collective-permute-done | bytes 262176 | tf_op jit(solution)/shard_map/ppermute | solution.py:25
  30.6 1.7 %collective-permute-start.8 = (bf16[512,256]{1,0:T(8,128)(2,1)S(1)}, bf16[512,256]{1,0:T(8,128)(2,1)S(1)}, u32[]{:S(2)}, u32[]{:S(2)}) collective-permute-start(bf16[512,256]{1,0:T(8,128)(2,1)S(1)} %collective-permute-done.7.refs_2_), channel_id=1, source_target_pairs={{0,1},{1,0},{2,3},{3,2},{4,5},{5,4},{6,7},{7,6},{8,9},{9,8},{10,11... | collective-permute-start | bytes 786440 | tf_op jit(solution)/shard_map/ppermute | solution.py:25
  33.5 5.5 %collective-permute-start.26 = (bf16[256,256]{1,0:T(8,128)(2,1)}, bf16[256,256]{1,0:T(8,128)(2,1)S(1)}, u32[]{:S(2)}, u32[]{:S(2)}) collective-permute-start(bf16[256,256]{1,0:T(8,128)(2,1)} %get-tuple-element.66), channel_id=1, source_target_pairs={{0,34},{1,35},{2,32},{3,33},{4,38},{5,39},{6,36},{7,37},{8,42},{9,... | collective-permute-start | bytes 393224 | tf_op jit(solution)/shard_map/ppermute | solution.py:25
  39.5 2.1 %shard_map.91 = (bf16[480,256]{1,0:T(8,128)(2,1)}, f32[8,256]{1,0:T(8,128)S(1)}, bf16[32,256]{1,0:T(8,128)(2,1)S(1)}, bf16[32,256]{1,0:T(8,128)(2,1)S(1)}) custom-call(bf16[2048,256]{1,0:T(8,128)(2,1)S(1)} %copy-done, bf16[2048,256]{1,0:T(8,128)(2,1)S(1)} %collective-permute-done.refs_1_, bf16[512,256]{1,0:T(8,128)(2,1)S(1)} %collective-permute-done.1.refs_2_, ...), custom_call_target="tpu_custom_call" | custom-call | flops 536870912 | bytes 4194304 | tf_op jit(solution)/shard_map/pallas_call | solution.py:195
  42.4 2.1 %shard_map.92 = (bf16[512,256]{1,0:T(8,128)(2,1)}, f32[8,256]{1,0:T(8,128)S(1)}, bf16[32,256]{1,0:T(8,128)(2,1)S(1)}) custom-call(bf16[2048,256]{1,0:T(8,128)(2,1)S(1)} %copy-done, bf16[2048,256]{1,0:T(8,128)(2,1)S(1)} %collective-permute-done.refs_1_, bf16[512,256]{1,0:T(8,128)(2,1)S(1)} %collective-permute-done.3.refs_2_, ...), custom_call_target="tpu_custom_call" | custom-call | flops 536870912 | bytes 4194304 | tf_op jit(solution)/shard_map/pallas_call | solution.py:195
  46.3 2.2 %shard_map.93 = (bf16[512,256]{1,0:T(8,128)(2,1)}, f32[8,256]{1,0:T(8,128)S(1)}, bf16[32,256]{1,0:T(8,128)(2,1)S(1)}) custom-call(bf16[2048,256]{1,0:T(8,128)(2,1)S(1)} %copy-done, bf16[2048,256]{1,0:T(8,128)(2,1)S(1)} %collective-permute-done.refs_1_, bf16[512,256]{1,0:T(8,128)(2,1)S(1)} %collective-permute-done.5.refs_2_, ...), custom_call_target="tpu_custom_call" | custom-call | flops 536870912 | bytes 4194304 | tf_op jit(solution)/shard_map/pallas_call | solution.py:195
  51.0 2.3 %shard_map.94 = (bf16[544,256]{1,0:T(8,128)(2,1)}, f32[8,256]{1,0:T(8,128)S(1)}, f32[64,4,128]{2,1,0:T(4,128)}) custom-call(bf16[2048,256]{1,0:T(8,128)(2,1)S(1)} %copy-done, bf16[2048,256]{1,0:T(8,128)(2,1)S(1)} %collective-permute-done.refs_1_, bf16[512,256]{1,0:T(8,128)(2,1)S(1)} %collective-permute-done.7.refs_2_, ...), custom_call_target="tpu_custom_call" | custom-call | flops 536870912 | bytes 4194304 | tf_op jit(solution)/shard_map/pallas_call | solution.py:195
  53.3 4.0 %collective-permute-done.28.refs_19_ = bf16[256,256]{1,0:T(8,128)(2,1)S(1)} collective-permute-done((bf16[256,256]{1,0:T(8,128)(2,1)S(1)}, bf16[256,256]{1,0:T(8,128)(2,1)S(1)}, u32[]{:S(2)}, u32[]{:S(2)}) %collective-permute-start.28) | collective-permute-done | bytes 131104 | tf_op jit(solution)/shard_map/ppermute | solution.py:25
  58.0 2.5 %collective-permute-done.29.refs_17_ = f32[8,256]{1,0:T(8,128)S(1)} collective-permute-done((f32[8,256]{1,0:T(8,128)S(1)}, f32[8,256]{1,0:T(8,128)S(1)}, u32[]{:S(2)}, u32[]{:S(2)}) %collective-permute-start.29) | collective-permute-done | bytes 8224 | tf_op jit(solution)/shard_map/ppermute | solution.py:25
  60.5 1.5 %collective-permute-start.15 = (bf16[512,256]{1,0:T(8,128)(2,1)S(1)}, bf16[512,256]{1,0:T(8,128)(2,1)S(1)}, u32[]{:S(2)}, u32[]{:S(2)}) collective-permute-start(bf16[512,256]{1,0:T(8,128)(2,1)S(1)} %copy-done.5), channel_id=1, source_target_pairs={{0,2},{1,3},{2,0},{3,1},{4,6},{5,7},{6,4},{7,5},{8,10},{9,11},{10,... | collective-permute-start | bytes 786440 | tf_op jit(solution)/shard_map/ppermute | solution.py:25
  62.7 1.9 %collective-permute-start.19 = (bf16[512,256]{1,0:T(8,128)(2,1)S(1)}, bf16[512,256]{1,0:T(8,128)(2,1)S(1)}, u32[]{:S(2)}, u32[]{:S(2)}) collective-permute-start(bf16[512,256]{1,0:T(8,128)(2,1)S(1)} %copy-done.5), channel_id=1, source_target_pairs={{0,1},{1,0},{2,3},{3,2},{4,5},{5,4},{6,7},{7,6},{8,9},{9,8},{10,11... | collective-permute-start | bytes 786440 | tf_op jit(solution)/shard_map/ppermute | solution.py:25
  65.1 2.4 %collective-permute-done.17.refs_7_ = bf16[544,256]{1,0:T(8,128)(2,1)S(1)} collective-permute-done((bf16[544,256]{1,0:T(8,128)(2,1)}, bf16[544,256]{1,0:T(8,128)(2,1)S(1)}, u32[]{:S(2)}, u32[]{:S(2)}) %collective-permute-start.17) | collective-permute-done | bytes 278560 | tf_op jit(solution)/shard_map/ppermute | solution.py:25
  67.5 4.1 %collective-permute-start.25 = (bf16[544,256]{1,0:T(8,128)(2,1)S(1)}, bf16[544,256]{1,0:T(8,128)(2,1)S(1)}, u32[]{:S(2)}, u32[]{:S(2)}) collective-permute-start(bf16[544,256]{1,0:T(8,128)(2,1)S(1)} %collective-permute-done.17.refs_7_), channel_id=1, source_target_pairs={{0,1},{1,0},{2,3},{3,2},{4,5},{5,4},{6,7},{7,6},{8,9},{9,8},{10,11... | collective-permute-start | bytes 835592 | tf_op jit(solution)/shard_map/ppermute | solution.py:25
  71.6 1.6 %collective-permute-done.15.refs_5_ = bf16[512,256]{1,0:T(8,128)(2,1)S(1)} collective-permute-done((bf16[512,256]{1,0:T(8,128)(2,1)S(1)}, bf16[512,256]{1,0:T(8,128)(2,1)S(1)}, u32[]{:S(2)}, u32[]{:S(2)}) %collective-permute-start.15) | collective-permute-done | bytes 262176 | tf_op jit(solution)/shard_map/ppermute | solution.py:25
  73.2 2.2 %collective-permute-start.24 = (bf16[512,256]{1,0:T(8,128)(2,1)S(1)}, bf16[512,256]{1,0:T(8,128)(2,1)S(1)}, u32[]{:S(2)}, u32[]{:S(2)}) collective-permute-start(bf16[512,256]{1,0:T(8,128)(2,1)S(1)} %collective-permute-done.16.refs_6_), channel_id=1, source_target_pairs={{0,1},{1,0},{2,3},{3,2},{4,5},{5,4},{6,7},{7,6},{8,9},{9,8},{10,11... | collective-permute-start | bytes 786440 | tf_op jit(solution)/shard_map/ppermute | solution.py:25
  75.4 8.1 %all-to-all-start = ((f32[64,4,128]{2,1,0:T(4,128)}), f32[64,4,128]{2,1,0:T(4,128)S(1)}, u32[]{:S(2)}, u32[]{:S(2)}) async-start(f32[64,4,128]{2,1,0:T(4,128)} %get-tuple-element.69), calls=%async_computation | async-start | bytes 262144 | tf_op jit(solution)/shard_map/all_to_all | solution.py:360
  85.3 9.7 %all-to-all-done.got = f32[64,4,128]{2,1,0:T(4,128)S(1)} async-done(((f32[64,4,128]{2,1,0:T(4,128)}), f32[64,4,128]{2,1,0:T(4,128)S(1)}, u32[]{:S(2)}, u32[]{:S(2)}) %all-to-all-start) | async-done | bytes 131104 | tf_op jit(solution)/shard_map/all_to_all | solution.py:360
  96.1 2.4 %collective-permute-start.33 = (f32[4,128]{1,0:T(4,128)S(1)}, f32[4,128]{1,0:T(4,128)S(1)}, u32[]{:S(2)}, u32[]{:S(2)}) collective-permute-start(f32[4,128]{1,0:T(4,128)S(1)} %combine.1.refs_20_), channel_id=1, source_target_pairs={{0,1},{1,0},{2,3},{3,2},{4,5},{5,4},{6,7},{7,6},{8,9},{9,8},{10,11... | collective-permute-start | bytes 6152 | tf_op jit(solution)/shard_map/ppermute | solution.py:25
  103.9 2.0 %hold.1 = (bf16[480,256]{1,0:T(8,128)(2,1)S(1)}, bf16[512,256]{1,0:T(8,128)(2,1)S(1)}, bf16[512,256]{1,0:T(8,128)(2,1)S(1)}, bf16[544,256]{1,0:T(8,128)(2,1)S(1)...) custom-call(bf16[480,256]{1,0:T(8,128)(2,1)S(1)} %copy-done.8, ...), custom_call_target="tpu_custom_call" | custom-call | tf_op jit(solution)/shard_map/hold/pallas_call | solution.py:375
  106.0 3.0 %finish.1 = bf16[2048,256]{1,0:T(8,128)(2,1)} custom-call(bf16[480,256]{1,0:T(8,128)(2,1)S(1)} %get-tuple-element.70.refs_0_, bf16[512,256]{1,0:T(8,128)(2,1)S(1)} %get-tuple-element.71.refs_1_, bf16[512,256]{1,0:T(8,128)(2,1)S(1)} %get-tuple-element.72.refs_2_, bf16[544,256]{1,0:T(8,128)(2,1)S(1)} %get-tuple-element.73.refs_3_, ...), custom_call_target="tpu_custom_call" | custom-call | flops 1073741824 | bytes 6291456 | tf_op jit(solution)/shard_map/finish/pallas_call | solution.py:389
  (134 shorter events, 26.0 us)
Async XLA Ops:
  0.0 38.9 %collective-permute-start = (bf16[2048,256]{1,0:T(8,128)(2,1)}, bf16[2048,256]{1,0:T(8,128)(2,1)S(1)}, u32[]{:S(2)}, u32[]{:S(2)}) collective-permute-start(bf16[2048,256]{1,0:T(8,128)(2,1)} %refs_0_.7), channel_id=1, source_target_pairs={{0,1},{1,0},{2,3},{3,2},{4,5},{5,4},{6,7},{7,6},{8,9},{9,8},{10,11... | collective-permute-start | bytes 3145736 | tf_op jit(solution)/shard_map/ppermute | solution.py:25
  4.2 19.7 %collective-permute-start.1 = (bf16[512,256]{1,0:T(8,128)(2,1)S(1)}, bf16[512,256]{1,0:T(8,128)(2,1)S(1)}, u32[]{:S(2)}, u32[]{:S(2)}) collective-permute-start(bf16[512,256]{1,0:T(8,128)(2,1)S(1)} %slice.48), channel_id=1, source_target_pairs={{0,2},{1,3},{2,0},{3,1},{4,6},{5,7},{6,4},{7,5},{8,10},{9,11},{10,... | collective-permute-start | bytes 786440 | tf_op jit(solution)/shard_map/ppermute | solution.py:25
  7.7 17.1 %collective-permute-start.3 = (bf16[512,256]{1,0:T(8,128)(2,1)S(1)}, bf16[512,256]{1,0:T(8,128)(2,1)S(1)}, u32[]{:S(2)}, u32[]{:S(2)}) collective-permute-start(bf16[512,256]{1,0:T(8,128)(2,1)S(1)} %get-tuple-element.95), channel_id=1, source_target_pairs={{0,2},{1,3},{2,0},{3,1},{4,6},{5,7},{6,4},{7,5},{8,10},{9,11},{10,... | collective-permute-start | bytes 786440 | tf_op jit(solution)/shard_map/ppermute | solution.py:25
  9.3 15.7 %collective-permute-start.5 = (bf16[512,256]{1,0:T(8,128)(2,1)S(1)}, bf16[512,256]{1,0:T(8,128)(2,1)S(1)}, u32[]{:S(2)}, u32[]{:S(2)}) collective-permute-start(bf16[512,256]{1,0:T(8,128)(2,1)S(1)} %get-tuple-element.94), channel_id=1, source_target_pairs={{0,2},{1,3},{2,0},{3,1},{4,6},{5,7},{6,4},{7,5},{8,10},{9,11},{10,... | collective-permute-start | bytes 786440 | tf_op jit(solution)/shard_map/ppermute | solution.py:25
  24.9 16.9 %collective-permute-start.4 = (bf16[512,256]{1,0:T(8,128)(2,1)S(1)}, bf16[512,256]{1,0:T(8,128)(2,1)S(1)}, u32[]{:S(2)}, u32[]{:S(2)}) collective-permute-start(bf16[512,256]{1,0:T(8,128)(2,1)S(1)} %collective-permute-done.3.refs_2_), channel_id=1, source_target_pairs={{0,1},{1,0},{2,3},{3,2},{4,5},{5,4},{6,7},{7,6},{8,9},{9,8},{10,11... | collective-permute-start | bytes 786440 | tf_op jit(solution)/shard_map/ppermute | solution.py:25
  24.9 20.6 %collective-permute-start.6 = (bf16[512,256]{1,0:T(8,128)(2,1)S(1)}, bf16[512,256]{1,0:T(8,128)(2,1)S(1)}, u32[]{:S(2)}, u32[]{:S(2)}) collective-permute-start(bf16[512,256]{1,0:T(8,128)(2,1)S(1)} %collective-permute-done.5.refs_2_), channel_id=1, source_target_pairs={{0,1},{1,0},{2,3},{3,2},{4,5},{5,4},{6,7},{7,6},{8,9},{9,8},{10,11... | collective-permute-start | bytes 786440 | tf_op jit(solution)/shard_map/ppermute | solution.py:25
  30.6 20.2 %collective-permute-start.8 = (bf16[512,256]{1,0:T(8,128)(2,1)S(1)}, bf16[512,256]{1,0:T(8,128)(2,1)S(1)}, u32[]{:S(2)}, u32[]{:S(2)}) collective-permute-start(bf16[512,256]{1,0:T(8,128)(2,1)S(1)} %collective-permute-done.7.refs_2_), channel_id=1, source_target_pairs={{0,1},{1,0},{2,3},{3,2},{4,5},{5,4},{6,7},{7,6},{8,9},{9,8},{10,11... | collective-permute-start | bytes 786440 | tf_op jit(solution)/shard_map/ppermute | solution.py:25
  33.5 15.0 %collective-permute-start.26 = (bf16[256,256]{1,0:T(8,128)(2,1)}, bf16[256,256]{1,0:T(8,128)(2,1)S(1)}, u32[]{:S(2)}, u32[]{:S(2)}) collective-permute-start(bf16[256,256]{1,0:T(8,128)(2,1)} %get-tuple-element.66), channel_id=1, source_target_pairs={{0,34},{1,35},{2,32},{3,33},{4,38},{5,39},{6,36},{7,37},{8,42},{9,... | collective-permute-start | bytes 393224 | tf_op jit(solution)/shard_map/ppermute | solution.py:25
  45.4 15.1 %collective-permute-start.14 = (bf16[480,256]{1,0:T(8,128)(2,1)S(1)}, bf16[480,256]{1,0:T(8,128)(2,1)}, u32[]{:S(2)}, u32[]{:S(2)}) collective-permute-start(bf16[480,256]{1,0:T(8,128)(2,1)S(1)} %copy-done.7), channel_id=1, source_target_pairs={{0,2},{1,3},{2,0},{3,1},{4,6},{5,7},{6,4},{7,5},{8,10},{9,11},{10,... | collective-permute-start | bytes 737288 | tf_op jit(solution)/shard_map/ppermute | solution.py:25
  45.5 16.4 %collective-permute-start.18 = (bf16[480,256]{1,0:T(8,128)(2,1)S(1)}, bf16[480,256]{1,0:T(8,128)(2,1)S(1)}, u32[]{:S(2)}, u32[]{:S(2)}) collective-permute-start(bf16[480,256]{1,0:T(8,128)(2,1)S(1)} %copy-done.7), channel_id=1, source_target_pairs={{0,1},{1,0},{2,3},{3,2},{4,5},{5,4},{6,7},{7,6},{8,9},{9,8},{10,11... | collective-permute-start | bytes 737288 | tf_op jit(solution)/shard_map/ppermute | solution.py:25
  49.1 15.5 %collective-permute-start.16 = (bf16[512,256]{1,0:T(8,128)(2,1)}, bf16[512,256]{1,0:T(8,128)(2,1)S(1)}, u32[]{:S(2)}, u32[]{:S(2)}) collective-permute-start(bf16[512,256]{1,0:T(8,128)(2,1)} %get-tuple-element.56.refs_2_), channel_id=1, source_target_pairs={{0,2},{1,3},{2,0},{3,1},{4,6},{5,7},{6,4},{7,5},{8,10},{9,11},{10,... | collective-permute-start | bytes 786440 | tf_op jit(solution)/shard_map/ppermute | solution.py:25
  50.5 14.1 %collective-permute-start.20 = (bf16[512,256]{1,0:T(8,128)(2,1)}, bf16[512,256]{1,0:T(8,128)(2,1)S(1)}, u32[]{:S(2)}, u32[]{:S(2)}) collective-permute-start(bf16[512,256]{1,0:T(8,128)(2,1)} %get-tuple-element.56.refs_2_), channel_id=1, source_target_pairs={{0,1},{1,0},{2,3},{3,2},{4,5},{5,4},{6,7},{7,6},{8,9},{9,8},{10,11... | collective-permute-start | bytes 786440 | tf_op jit(solution)/shard_map/ppermute | solution.py:25
  60.5 12.7 %collective-permute-start.15 = (bf16[512,256]{1,0:T(8,128)(2,1)S(1)}, bf16[512,256]{1,0:T(8,128)(2,1)S(1)}, u32[]{:S(2)}, u32[]{:S(2)}) collective-permute-start(bf16[512,256]{1,0:T(8,128)(2,1)S(1)} %copy-done.5), channel_id=1, source_target_pairs={{0,2},{1,3},{2,0},{3,1},{4,6},{5,7},{6,4},{7,5},{8,10},{9,11},{10,... | collective-permute-start | bytes 786440 | tf_op jit(solution)/shard_map/ppermute | solution.py:25
  62.7 12.7 %collective-permute-start.19 = (bf16[512,256]{1,0:T(8,128)(2,1)S(1)}, bf16[512,256]{1,0:T(8,128)(2,1)S(1)}, u32[]{:S(2)}, u32[]{:S(2)}) collective-permute-start(bf16[512,256]{1,0:T(8,128)(2,1)S(1)} %copy-done.5), channel_id=1, source_target_pairs={{0,1},{1,0},{2,3},{3,2},{4,5},{5,4},{6,7},{7,6},{8,9},{9,8},{10,11... | collective-permute-start | bytes 786440 | tf_op jit(solution)/shard_map/ppermute | solution.py:25
  64.6 18.9 %collective-permute-start.21 = (bf16[544,256]{1,0:T(8,128)(2,1)}, bf16[544,256]{1,0:T(8,128)(2,1)S(1)}, u32[]{:S(2)}, u32[]{:S(2)}) collective-permute-start(bf16[544,256]{1,0:T(8,128)(2,1)} %get-tuple-element.64.refs_3_), channel_id=1, source_target_pairs={{0,1},{1,0},{2,3},{3,2},{4,5},{5,4},{6,7},{7,6},{8,9},{9,8},{10,11... | collective-permute-start | bytes 835592 | tf_op jit(solution)/shard_map/ppermute | solution.py:25
  64.6 19.8 %collective-permute-start.22 = (bf16[480,256]{1,0:T(8,128)(2,1)}, bf16[480,256]{1,0:T(8,128)(2,1)}, u32[]{:S(2)}, u32[]{:S(2)}) collective-permute-start(bf16[480,256]{1,0:T(8,128)(2,1)} %collective-permute-done.14.refs_4_), channel_id=1, source_target_pairs={{0,1},{1,0},{2,3},{3,2},{4,5},{5,4},{6,7},{7,6},{8,9},{9,8},{10,11... | collective-permute-start | bytes 737288 | tf_op jit(solution)/shard_map/ppermute | solution.py:25
  67.5 31.0 %collective-permute-start.25 = (bf16[544,256]{1,0:T(8,128)(2,1)S(1)}, bf16[544,256]{1,0:T(8,128)(2,1)S(1)}, u32[]{:S(2)}, u32[]{:S(2)}) collective-permute-start(bf16[544,256]{1,0:T(8,128)(2,1)S(1)} %collective-permute-done.17.refs_7_), channel_id=1, source_target_pairs={{0,1},{1,0},{2,3},{3,2},{4,5},{5,4},{6,7},{7,6},{8,9},{9,8},{10,11... | collective-permute-start | bytes 835592 | tf_op jit(solution)/shard_map/ppermute | solution.py:25
  73.2 22.0 %collective-permute-start.24 = (bf16[512,256]{1,0:T(8,128)(2,1)S(1)}, bf16[512,256]{1,0:T(8,128)(2,1)S(1)}, u32[]{:S(2)}, u32[]{:S(2)}) collective-permute-start(bf16[512,256]{1,0:T(8,128)(2,1)S(1)} %collective-permute-done.16.refs_6_), channel_id=1, source_target_pairs={{0,1},{1,0},{2,3},{3,2},{4,5},{5,4},{6,7},{7,6},{8,9},{9,8},{10,11... | collective-permute-start | bytes 786440 | tf_op jit(solution)/shard_map/ppermute | solution.py:25
  75.4 20.7 %collective-permute-start.23 = (bf16[512,256]{1,0:T(8,128)(2,1)S(1)}, bf16[512,256]{1,0:T(8,128)(2,1)S(1)}, u32[]{:S(2)}, u32[]{:S(2)}) collective-permute-start(bf16[512,256]{1,0:T(8,128)(2,1)S(1)} %collective-permute-done.15.refs_5_), channel_id=1, source_target_pairs={{0,1},{1,0},{2,3},{3,2},{4,5},{5,4},{6,7},{7,6},{8,9},{9,8},{10,11... | collective-permute-start | bytes 786440 | tf_op jit(solution)/shard_map/ppermute | solution.py:25
  75.4 19.6 %all-to-all-start = ((f32[64,4,128]{2,1,0:T(4,128)}), f32[64,4,128]{2,1,0:T(4,128)S(1)}, u32[]{:S(2)}, u32[]{:S(2)}) async-start(f32[64,4,128]{2,1,0:T(4,128)} %get-tuple-element.69), calls=%async_computation | async-start | bytes 262144 | tf_op jit(solution)/shard_map/all_to_all | solution.py:360
  83.5 22.4 %collective-permute-start.30 = (f32[8,256]{1,0:T(8,128)S(1)}, f32[8,256]{1,0:T(8,128)S(1)}, u32[]{:S(2)}, u32[]{:S(2)}) collective-permute-start(f32[8,256]{1,0:T(8,128)S(1)} %get-tuple-element.86.refs_16_), channel_id=1, source_target_pairs={{0,1},{1,0},{2,3},{3,2},{4,5},{5,4},{6,7},{7,6},{8,9},{9,8},{10,11... | collective-permute-start | bytes 24584 | tf_op jit(solution)/shard_map/ppermute | solution.py:25
  84.4 21.6 %collective-permute-start.31 = (f32[8,256]{1,0:T(8,128)S(1)}, f32[8,256]{1,0:T(8,128)S(1)}, u32[]{:S(2)}, u32[]{:S(2)}) collective-permute-start(f32[8,256]{1,0:T(8,128)S(1)} %get-tuple-element.86.refs_16_), channel_id=1, source_target_pairs={{0,3},{1,2},{2,1},{3,0},{4,7},{5,6},{6,5},{7,4},{8,11},{9,10},{10,... | collective-permute-start | bytes 24584 | tf_op jit(solution)/shard_map/ppermute | solution.py:25
  95.2 10.8 %collective-permute-start.32 = (f32[4,128]{1,0:T(4,128)S(1)}, f32[4,128]{1,0:T(4,128)S(1)}, u32[]{:S(2)}, u32[]{:S(2)}) collective-permute-start(f32[4,128]{1,0:T(4,128)S(1)} %combine.1.refs_20_), channel_id=1, source_target_pairs={{0,2},{1,3},{2,0},{3,1},{4,6},{5,7},{6,4},{7,5},{8,10},{9,11},{10,... | collective-permute-start | bytes 6152 | tf_op jit(solution)/shard_map/ppermute | solution.py:25
  96.1 9.9 %collective-permute-start.33 = (f32[4,128]{1,0:T(4,128)S(1)}, f32[4,128]{1,0:T(4,128)S(1)}, u32[]{:S(2)}, u32[]{:S(2)}) collective-permute-start(f32[4,128]{1,0:T(4,128)S(1)} %combine.1.refs_20_), channel_id=1, source_target_pairs={{0,1},{1,0},{2,3},{3,2},{4,5},{5,4},{6,7},{7,6},{8,9},{9,8},{10,11... | collective-permute-start | bytes 6152 | tf_op jit(solution)/shard_map/ppermute | solution.py:25
  (39 other events, 461.9 us)
where the time goes:
time: 109 us
  starting transfers between devices  47.6 us (44%)
  waiting for transfers between devices  34.5 us (32%)
  Pallas kernels  14.7 us (13%)
  local copies, waits for them, and re-layouts  11.7 us (11%)
    ppermute x35, starting transfers between devices, permute(): return lax.ppermute(value, AXES, pairs)  39.5 us
    ppermute x35, waiting for transfers between devices, permute(): return lax.ppermute(value, AXES, pairs)  24.8 us
    all_to_all x1, waiting for transfers between devices, body(): got = lax.all_to_all(sent, 'tm', 0, 0)  9.74 us
    pallas_call x4, Pallas kernels, stage_call(): pl.pallas_call(functools.partial(stage_kernel, stage, taps_count, rows, e...  8.66 us
    all_to_all x1, starting transfers between devices, body(): got = lax.all_to_all(sent, 'tm', 0, 0)  8.11 us
    unnamed x51, local copies, waits for them, and re-layouts  7.32 us
    pallas_call x1, Pallas kernels, body(): pl.pallas_call(functools.partial(finish_kernel, 4, bounds), out_shape=jax...  2.97 us
  transfers between devices with their start and end apart: 36, of which 9 were waited for; matrix products, arithmetic and copies ran while one was open for 4% of the time, Pallas kernels for 11%

commit v1 on v0

--- a/solution.py
+++ b/solution.py
@@ -104,7 +104,7 @@
 
     def conv_rows(source, target, row, sums):
         frame = line + row
-        lo, hi = start[pl.ds(target, STEP), :] - frame, end[pl.ds(target, STEP), :] - frame
+        lo, hi = start[pl.ds(row, STEP), :] - frame, end[pl.ds(row, STEP), :] - frame
         out = []
         for j in range(blocks):
             acc = None
@@ -169,12 +169,11 @@
             sent_out[i] = piece
 
 
-UNROLL = 4
-
-
-def stage_call(stage, taps_count, rows, edge, devices, xs, halos, weights, taps, start, end, tail, head, earlier):
+UNROLL = 8
+
+
+def stage_call(stage, taps_count, rows, edge, count, devices, xs, halos, weights, taps, start, end, tail, head, earlier):
     fresh, width = xs[2].shape[0], weights[0].shape[1]
-    count = start.shape[0]
     margin = pltpu.VMEM((TAIL, width), BF16)
     outs = [pltpu.HBM((count, width), BF16), pltpu.VMEM((8, width), F32)]
     operands = list(xs)
@@ -224,14 +223,18 @@
         outs[i][...] = down[:, pl.ds(pl.multiple_of((chan ^ i) * width, width), width)]
 
 
-def combine_kernel(rows, total, got, gain, shift, out):
+def combine_kernel(rows, total, pieces, got, gain, shift, centres, out):
     half = gain.shape[0]
     means = got[:, 0:half, :]
     mean = jnp.sum(means, axis=0) * (1.0 / got.shape[0])
     var = jnp.sum(got[:, half:, :] + rows * (means - mean) ** 2, axis=0) * (1.0 / total)
     scale = gain[...] / jnp.sqrt(var + 1e-05)
     out[0:half, :] = scale
-    out[half:, :] = shift[...] - mean * scale
+    for piece in range(pieces):
+        for j in range(half):
+            centre = centres[piece : piece + 1, j * LANES : (j + 1) * LANES]
+            at = (piece + 1) * half + j
+            out[at : at + 1, :] = shift[j : j + 1, :] + (centre - mean[j : j + 1]) * scale[j : j + 1]
 
 
 def hold_kernel(*refs):
@@ -246,7 +249,7 @@
 
 def finish_kernel(pieces, bounds, *refs):
     held, refs = refs[: 4 * pieces], refs[4 * pieces :]
-    means, scales, weights, out = refs[:4], refs[4:8], refs[8:12], refs[12]
+    scales, weights, out = refs[:4], refs[4:8], refs[8]
     width = out.shape[1]
     for piece in range(pieces):
         parts = []
@@ -254,8 +257,8 @@
             for j in range(width // LANES):
                 cut = slice(j * LANES, (j + 1) * LANES)
                 a = scales[block][j : j + 1, :] * 0.5
-                b = scales[block][width // LANES + j : width // LANES + j + 1, :] * 0.5
-                b = b + means[block][piece : piece + 1, cut] * a
+                at = (piece + 1) * (width // LANES) + j
+                b = scales[block][at : at + 1, :] * 0.5
                 h = held[block * pieces + piece][:, cut].astype(F32) * a + b
                 parts.append((h + h * jnp.tanh(h)).astype(BF16))
         swished = jnp.concatenate(parts, axis=1)
@@ -324,21 +327,15 @@
 
     edges = [16, chunk - 16, 2 * chunk - 16, 3 * chunk - 16, rows]
 
-    def spread(vector, k):
-        part = vector[edges[k] : edges[k + 1]]
-        if k == 3:
-            part = jnp.concatenate([part, vector[:16]])
-        return jnp.broadcast_to(part[:, None], (part.shape[0], LANES))
-
-    starts, ends = [spread(rec_start, k) for k in range(4)], [spread(rec_end, k) for k in range(4)]
+    counts = [edges[k + 1] - edges[k] for k in range(3)] + [rows - edges[3] + 16]
+    start = jnp.broadcast_to(rec_start[:, None], (rows, LANES))
+    end = jnp.broadcast_to(rec_end[:, None], (rows, LANES))
 
     convs, stats, tail, head = [], [], None, None
     for k in range(4):
-        if k == 2:
-            tail, starts[3], ends[3] = lax.optimization_barrier((tail, starts[3], ends[3]))
         out = stage_call(
-            k, taps_count, rows, edges[k], tms, [features, mate, linked[k], far[k]], halos, weights, taps,
-            starts[k], ends[k], tail, head, stats,
+            k, taps_count, rows, edges[k], counts[k], tms, [features, mate, linked[k], far[k]], halos, weights, taps,
+            start, end, tail, head, stats,
         )
         convs.append(out[0])
         stats.append(out[1])
@@ -353,20 +350,21 @@
 
     pieces = [spread_out(k) for k in range(4)]
     convs = [pieces[k][block] for block in range(4) for k in range(4)]
-    means = [stats[3]]
-    for move in (over_link, to_core, to_diagonal):
-        means.append(permute(stats[3], move))
-
     got = lax.all_to_all(sent, "tm", 0, 0)
     half = width // LANES
     own_scale = pl.pallas_call(
-        functools.partial(combine_kernel, float(rows), float(total)),
-        out_shape=pltpu.VMEM((2 * half, LANES), F32),
-        in_specs=[vmem] * 3,
+        functools.partial(combine_kernel, float(rows), float(total), 4),
+        out_shape=pltpu.VMEM((16, LANES), F32),
+        in_specs=[vmem] * 4,
         out_specs=vmem,
         compiler_params=pltpu.CompilerParams(vmem_limit_bytes=4 << 20),
         name="combine",
-    )(near(got), near(norm_gain.astype(F32).reshape(half, LANES)), near(norm_shift.astype(F32).reshape(half, LANES)))
+    )(
+        near(got),
+        near(norm_gain.astype(F32).reshape(half, LANES)),
+        near(norm_shift.astype(F32).reshape(half, LANES)),
+        near(stats[3]),
+    )
     scales = [own_scale]
     for move in (over_link, to_core, to_diagonal):
         scales.append(permute(own_scale, move))
@@ -385,7 +383,7 @@
 
     bounds = [[(edges[k], edges[k + 1] - edges[k])] for k in range(4)]
     bounds[3].append((0, 16))
-    operands = [near(o) for o in [*convs, *means, *scales, *down]]
+    operands = [near(o) for o in [*convs, *scales, *down]]
     return pl.pallas_call(
         functools.partial(finish_kernel, 4, bounds),
         out_shape=jax.ShapeDtypeStruct((rows, width), BF16),

time: 109 us -> 109 us (level)
  waiting for transfers between devices: 34.5 us -> 30.1 us
  starting transfers between devices: 47.6 us -> 50.4 us
    ppermute x35 -> x32, waiting for transfers between devices: 24.8 us -> 18.8 us  [permute(): return lax.ppermute(value, AXES, pairs)]
    all_to_all x1, starting transfers between devices: 8.11 us -> 12.3 us  [body(): got = lax.all_to_all(sent, 'tm', 0, 0)]
    all_to_all x1, waiting for transfers between devices: 9.74 us -> 11.3 us  [body(): got = lax.all_to_all(sent, 'tm', 0, 0)]
    unnamed x51 -> x49, local copies, waits for them, and re-layouts: 7.32 us -> 8.81 us
    ppermute x35 -> x32, starting transfers between devices: 39.5 us -> 38.1 us  [permute(): return lax.ppermute(value, AXES, pairs)]
  transfers between devices with their start and end apart: 36 -> 33, of which waited for: 9 -> 6; matrix products, arithmetic and copies ran while one was open for 4% -> 3% of each run, Pallas kernels for 11% -> 11%
where the time goes in v1:
time: 109 us; the launch traced here: 108 us
  starting transfers between devices  50.4 us (46%)
  waiting for transfers between devices  30.1 us (28%)
  Pallas kernels  15 us (14%)
  local copies, waits for them, and re-layouts  12.3 us (11%)
    ppermute x32, starting transfers between devices, permute(): return lax.ppermute(value, AXES, pairs)  38.1 us
    ppermute x32, waiting for transfers between devices, permute(): return lax.ppermute(value, AXES, pairs)  18.8 us
    all_to_all x1, starting transfers between devices, body(): got = lax.all_to_all(sent, 'tm', 0, 0)  12.3 us
    all_to_all x1, waiting for transfers between devices, body(): got = lax.all_to_all(sent, 'tm', 0, 0)  11.3 us
    unnamed x49, local copies, waits for them, and re-layouts  8.81 us
    pallas_call x4, Pallas kernels, stage_call(): pl.pallas_call(functools.partial(stage_kernel, stage, taps_count, rows, e...  8.59 us
    pallas_call x1, Pallas kernels, body(): pl.pallas_call(functools.partial(finish_kernel, 4, bounds), out_shape=jax...  2.93 us
    pallas_call x1, Pallas kernels, body(): pl.pallas_call(hold_kernel, out_shape=[pltpu.VMEM(c.shape, c.dtype) for c...  2.31 us
  transfers between devices with their start and end apart: 33, of which 6 were waited for; matrix products, arithmetic and copies ran while one was open for 3% of the time, Pallas kernels for 11%

profile of v1, /device:TPU:1, one launch (start us, length us, event | category | flops | bytes accessed | tf_op | source)
XLA Modules:
  0.0 108.1 jit_solution(6665452536795901301)
XLA Ops:
  0.0 3.2 %collective-permute-start = (bf16[2048,256]{1,0:T(8,128)(2,1)}, bf16[2048,256]{1,0:T(8,128)(2,1)S(1)}, u32[]{:S(2)}, u32[]{:S(2)}) collective-permute-start(bf16[2048,256]{1,0:T(8,128)(2,1)} %refs_0_.7), channel_id=1, source_target_pairs={{0,1},{1,0},{2,3},{3,2},{4,5},{5,4},{6,7},{7,6},{8,9},{9,8},{10,11... | collective-permute-start | bytes 3145736 | tf_op jit(solution)/shard_map/ppermute | solution.py:25
  6.3 4.1 %collective-permute-start.10 = (bf16[8,256]{1,0:T(8,128)(2,1)S(1)}, bf16[8,256]{1,0:T(8,128)(2,1)S(1)}, u32[]{:S(2)}, u32[]{:S(2)}) collective-permute-start(bf16[8,256]{1,0:T(8,128)(2,1)S(1)} %get-tuple-element.85), channel_id=1, source_target_pairs={{0,4},{1,5},{2,6},{3,7},{4,8},{5,9},{6,10},{7,11},{8,12},{9,13},{1... | collective-permute-start | bytes 12296 | tf_op jit(solution)/shard_map/ppermute | solution.py:25
  11.6 1.5 %collective-permute-start.3 = (bf16[512,256]{1,0:T(8,128)(2,1)S(1)}, bf16[512,256]{1,0:T(8,128)(2,1)S(1)}, u32[]{:S(2)}, u32[]{:S(2)}) collective-permute-start(bf16[512,256]{1,0:T(8,128)(2,1)S(1)} %get-tuple-element.89), channel_id=1, source_target_pairs={{0,2},{1,3},{2,0},{3,1},{4,6},{5,7},{6,4},{7,5},{8,10},{9,11},{10,... | collective-permute-start | bytes 786440 | tf_op jit(solution)/shard_map/ppermute | solution.py:25
  14.6 1.7 %collective-permute-start.2 = (bf16[512,256]{1,0:T(8,128)(2,1)S(1)}, bf16[512,256]{1,0:T(8,128)(2,1)S(1)}, u32[]{:S(2)}, u32[]{:S(2)}) collective-permute-start(bf16[512,256]{1,0:T(8,128)(2,1)S(1)} %collective-permute-done.1.refs_2_), channel_id=1, source_target_pairs={{0,1},{1,0},{2,3},{3,2},{4,5},{5,4},{6,7},{7,6},{8,9},{9,8},{10,11... | collective-permute-start | bytes 786440 | tf_op jit(solution)/shard_map/ppermute | solution.py:25
  16.4 2.6 %collective-permute-done.3.refs_2_ = bf16[512,256]{1,0:T(8,128)(2,1)S(1)} collective-permute-done((bf16[512,256]{1,0:T(8,128)(2,1)S(1)}, bf16[512,256]{1,0:T(8,128)(2,1)S(1)}, u32[]{:S(2)}, u32[]{:S(2)}) %collective-permute-start.3) | collective-permute-done | bytes 262176 | tf_op jit(solution)/shard_map/ppermute | solution.py:25
  19.0 2.5 %collective-permute-start.4 = (bf16[512,256]{1,0:T(8,128)(2,1)S(1)}, bf16[512,256]{1,0:T(8,128)(2,1)S(1)}, u32[]{:S(2)}, u32[]{:S(2)}) collective-permute-start(bf16[512,256]{1,0:T(8,128)(2,1)S(1)} %collective-permute-done.3.refs_2_), channel_id=1, source_target_pairs={{0,1},{1,0},{2,3},{3,2},{4,5},{5,4},{6,7},{7,6},{8,9},{9,8},{10,11... | collective-permute-start | bytes 786440 | tf_op jit(solution)/shard_map/ppermute | solution.py:25
  21.5 3.2 %collective-permute-done.5.refs_2_ = bf16[512,256]{1,0:T(8,128)(2,1)S(1)} collective-permute-done((bf16[512,256]{1,0:T(8,128)(2,1)S(1)}, bf16[512,256]{1,0:T(8,128)(2,1)S(1)}, u32[]{:S(2)}, u32[]{:S(2)}) %collective-permute-start.5) | collective-permute-done | bytes 262176 | tf_op jit(solution)/shard_map/ppermute | solution.py:25
  24.7 2.4 %collective-permute-start.6 = (bf16[512,256]{1,0:T(8,128)(2,1)S(1)}, bf16[512,256]{1,0:T(8,128)(2,1)S(1)}, u32[]{:S(2)}, u32[]{:S(2)}) collective-permute-start(bf16[512,256]{1,0:T(8,128)(2,1)S(1)} %collective-permute-done.5.refs_2_), channel_id=1, source_target_pairs={{0,1},{1,0},{2,3},{3,2},{4,5},{5,4},{6,7},{7,6},{8,9},{9,8},{10,11... | collective-permute-start | bytes 786440 | tf_op jit(solution)/shard_map/ppermute | solution.py:25
  27.1 3.2 %collective-permute-done.7.refs_2_ = bf16[512,256]{1,0:T(8,128)(2,1)S(1)} collective-permute-done((bf16[512,256]{1,0:T(8,128)(2,1)S(1)}, bf16[512,256]{1,0:T(8,128)(2,1)S(1)}, u32[]{:S(2)}, u32[]{:S(2)}) %collective-permute-start.7) | collective-permute-done | bytes 262176 | tf_op jit(solution)/shard_map/ppermute | solution.py:25
  30.3 1.4 %collective-permute-start.8 = (bf16[512,256]{1,0:T(8,128)(2,1)S(1)}, bf16[512,256]{1,0:T(8,128)(2,1)S(1)}, u32[]{:S(2)}, u32[]{:S(2)}) collective-permute-start(bf16[512,256]{1,0:T(8,128)(2,1)S(1)} %collective-permute-done.7.refs_2_), channel_id=1, source_target_pairs={{0,1},{1,0},{2,3},{3,2},{4,5},{5,4},{6,7},{7,6},{8,9},{9,8},{10,11... | collective-permute-start | bytes 786440 | tf_op jit(solution)/shard_map/ppermute | solution.py:25
  31.7 1.4 %collective-permute-start.12 = (bf16[16,256]{1,0:T(8,128)(2,1)S(1)}, bf16[16,256]{1,0:T(8,128)(2,1)S(1)}, u32[]{:S(2)}, u32[]{:S(2)}) collective-permute-start(bf16[16,256]{1,0:T(8,128)(2,1)S(1)} %constant_dynamic-update-slice_fusion.refs_4_), channel_id=1, source_target_pairs={{0,2},{1,3},{2,0},{3,1},{4,6},{5,7},{6,4},{7,5},{8,10},{9,11},{10,... | collective-permute-start | bytes 24584 | tf_op jit(solution)/shard_map/ppermute | solution.py:25
  34.8 2.1 %shard_map.91 = (bf16[480,256]{1,0:T(8,128)(2,1)}, f32[8,256]{1,0:T(8,128)S(1)}, bf16[32,256]{1,0:T(8,128)(2,1)S(1)}, bf16[32,256]{1,0:T(8,128)(2,1)S(1)}) custom-call(bf16[2048,256]{1,0:T(8,128)(2,1)S(1)} %copy-done, bf16[2048,256]{1,0:T(8,128)(2,1)S(1)} %collective-permute-done.refs_1_, bf16[512,256]{1,0:T(8,128)(2,1)S(1)} %collective-permute-done.1.refs_2_, ...), custom_call_target="tpu_custom_call" | custom-call | flops 536870912 | bytes 4194304 | tf_op jit(solution)/shard_map/pallas_call | solution.py:194
  39.6 5.8 %collective-permute-start.26 = (bf16[256,256]{1,0:T(8,128)(2,1)}, bf16[256,256]{1,0:T(8,128)(2,1)S(1)}, u32[]{:S(2)}, u32[]{:S(2)}) collective-permute-start(bf16[256,256]{1,0:T(8,128)(2,1)} %get-tuple-element.60), channel_id=1, source_target_pairs={{0,34},{1,35},{2,32},{3,33},{4,38},{5,39},{6,36},{7,37},{8,42},{9,... | collective-permute-start | bytes 393224 | tf_op jit(solution)/shard_map/ppermute | solution.py:25
  45.9 2.1 %shard_map.92 = (bf16[512,256]{1,0:T(8,128)(2,1)}, f32[8,256]{1,0:T(8,128)S(1)}, bf16[32,256]{1,0:T(8,128)(2,1)S(1)}) custom-call(bf16[2048,256]{1,0:T(8,128)(2,1)S(1)} %copy-done, bf16[2048,256]{1,0:T(8,128)(2,1)S(1)} %collective-permute-done.refs_1_, bf16[512,256]{1,0:T(8,128)(2,1)S(1)} %collective-permute-done.3.refs_2_, ...), custom_call_target="tpu_custom_call" | custom-call | flops 536870912 | bytes 4194304 | tf_op jit(solution)/shard_map/pallas_call | solution.py:194
  48.0 2.1 %shard_map.93 = (bf16[512,256]{1,0:T(8,128)(2,1)}, f32[8,256]{1,0:T(8,128)S(1)}, bf16[32,256]{1,0:T(8,128)(2,1)S(1)}) custom-call(bf16[2048,256]{1,0:T(8,128)(2,1)S(1)} %copy-done, bf16[2048,256]{1,0:T(8,128)(2,1)S(1)} %collective-permute-done.refs_1_, bf16[512,256]{1,0:T(8,128)(2,1)S(1)} %collective-permute-done.5.refs_2_, ...), custom_call_target="tpu_custom_call" | custom-call | flops 536870912 | bytes 4194304 | tf_op jit(solution)/shard_map/pallas_call | solution.py:194
  50.1 2.2 %shard_map.94 = (bf16[544,256]{1,0:T(8,128)(2,1)}, f32[8,256]{1,0:T(8,128)S(1)}, f32[64,4,128]{2,1,0:T(4,128)}) custom-call(bf16[2048,256]{1,0:T(8,128)(2,1)S(1)} %copy-done, bf16[2048,256]{1,0:T(8,128)(2,1)S(1)} %collective-permute-done.refs_1_, bf16[512,256]{1,0:T(8,128)(2,1)S(1)} %collective-permute-done.7.refs_2_, ...), custom_call_target="tpu_custom_call" | custom-call | flops 536870912 | bytes 4194304 | tf_op jit(solution)/shard_map/pallas_call | solution.py:194
  53.7 1.4 %collective-permute-start.16 = (bf16[512,256]{1,0:T(8,128)(2,1)S(1)}, bf16[512,256]{1,0:T(8,128)(2,1)S(1)}, u32[]{:S(2)}, u32[]{:S(2)}) collective-permute-start(bf16[512,256]{1,0:T(8,128)(2,1)S(1)} %copy-done.6), channel_id=1, source_target_pairs={{0,2},{1,3},{2,0},{3,1},{4,6},{5,7},{6,4},{7,5},{8,10},{9,11},{10,... | collective-permute-start | bytes 786440 | tf_op jit(solution)/shard_map/ppermute | solution.py:25
  57.8 9.0 %collective-permute-done.16.refs_6_ = bf16[512,256]{1,0:T(8,128)(2,1)S(1)} collective-permute-done((bf16[512,256]{1,0:T(8,128)(2,1)S(1)}, bf16[512,256]{1,0:T(8,128)(2,1)S(1)}, u32[]{:S(2)}, u32[]{:S(2)}) %collective-permute-start.16) | collective-permute-done | bytes 262176 | tf_op jit(solution)/shard_map/ppermute | solution.py:25
  66.8 1.9 %collective-permute-start.21 = (bf16[544,256]{1,0:T(8,128)(2,1)}, bf16[544,256]{1,0:T(8,128)(2,1)S(1)}, u32[]{:S(2)}, u32[]{:S(2)}) collective-permute-start(bf16[544,256]{1,0:T(8,128)(2,1)} %get-tuple-element.58.refs_3_), channel_id=1, source_target_pairs={{0,1},{1,0},{2,3},{3,2},{4,5},{5,4},{6,7},{7,6},{8,9},{9,8},{10,11... | collective-permute-start | bytes 835592 | tf_op jit(solution)/shard_map/ppermute | solution.py:25
  69.2 12.3 %all-to-all-start = ((f32[64,4,128]{2,1,0:T(4,128)}), f32[64,4,128]{2,1,0:T(4,128)S(1)}, u32[]{:S(2)}, u32[]{:S(2)}) async-start(f32[64,4,128]{2,1,0:T(4,128)} %get-tuple-element.63), calls=%async_computation | async-start | bytes 262144 | tf_op jit(solution)/shard_map/all_to_all | solution.py:353
  82.1 11.3 %all-to-all-done.got = f32[64,4,128]{2,1,0:T(4,128)S(1)} async-done(((f32[64,4,128]{2,1,0:T(4,128)}), f32[64,4,128]{2,1,0:T(4,128)S(1)}, u32[]{:S(2)}, u32[]{:S(2)}) %all-to-all-start) | async-done | bytes 131104 | tf_op jit(solution)/shard_map/all_to_all | solution.py:353
  94.7 1.9 %collective-permute-start.30 = (f32[16,128]{1,0:T(8,128)S(1)}, f32[16,128]{1,0:T(8,128)S(1)}, u32[]{:S(2)}, u32[]{:S(2)}) collective-permute-start(f32[16,128]{1,0:T(8,128)S(1)} %combine.1.refs_20_.refs_16_), channel_id=1, source_target_pairs={{0,1},{1,0},{2,3},{3,2},{4,5},{5,4},{6,7},{7,6},{8,9},{9,8},{10,11... | collective-permute-start | bytes 24584 | tf_op jit(solution)/shard_map/ppermute | solution.py:25
  102.8 2.3 %hold.1 = (bf16[480,256]{1,0:T(8,128)(2,1)S(1)}, bf16[512,256]{1,0:T(8,128)(2,1)S(1)}, bf16[512,256]{1,0:T(8,128)(2,1)S(1)}, bf16[544,256]{1,0:T(8,128)(2,1)S(1)...) custom-call(bf16[480,256]{1,0:T(8,128)(2,1)S(1)} %copy-done.7, ...), custom_call_target="tpu_custom_call" | custom-call | tf_op jit(solution)/shard_map/hold/pallas_call | solution.py:373
  105.2 2.9 %finish.1 = bf16[2048,256]{1,0:T(8,128)(2,1)} custom-call(bf16[480,256]{1,0:T(8,128)(2,1)S(1)} %get-tuple-element.65.refs_0_, bf16[512,256]{1,0:T(8,128)(2,1)S(1)} %get-tuple-element.66.refs_1_, bf16[512,256]{1,0:T(8,128)(2,1)S(1)} %get-tuple-element.67.refs_2_, bf16[544,256]{1,0:T(8,128)(2,1)S(1)} %get-tuple-element.68.refs_3_, ...), custom_call_target="tpu_custom_call" | custom-call | flops 1073741824 | bytes 6291456 | tf_op jit(solution)/shard_map/finish/pallas_call | solution.py:387
  (108 shorter events, 23.2 us)
Async XLA Ops:
  0.0 33.2 %collective-permute-start = (bf16[2048,256]{1,0:T(8,128)(2,1)}, bf16[2048,256]{1,0:T(8,128)(2,1)S(1)}, u32[]{:S(2)}, u32[]{:S(2)}) collective-permute-start(bf16[2048,256]{1,0:T(8,128)(2,1)} %refs_0_.7), channel_id=1, source_target_pairs={{0,1},{1,0},{2,3},{3,2},{4,5},{5,4},{6,7},{7,6},{8,9},{9,8},{10,11... | collective-permute-start | bytes 3145736 | tf_op jit(solution)/shard_map/ppermute | solution.py:25
  4.2 10.4 %collective-permute-start.1 = (bf16[512,256]{1,0:T(8,128)(2,1)S(1)}, bf16[512,256]{1,0:T(8,128)(2,1)S(1)}, u32[]{:S(2)}, u32[]{:S(2)}) collective-permute-start(bf16[512,256]{1,0:T(8,128)(2,1)S(1)} %slice.18), channel_id=1, source_target_pairs={{0,2},{1,3},{2,0},{3,1},{4,6},{5,7},{6,4},{7,5},{8,10},{9,11},{10,... | collective-permute-start | bytes 786440 | tf_op jit(solution)/shard_map/ppermute | solution.py:25
  13.1 11.6 %collective-permute-start.5 = (bf16[512,256]{1,0:T(8,128)(2,1)S(1)}, bf16[512,256]{1,0:T(8,128)(2,1)S(1)}, u32[]{:S(2)}, u32[]{:S(2)}) collective-permute-start(bf16[512,256]{1,0:T(8,128)(2,1)S(1)} %get-tuple-element.88), channel_id=1, source_target_pairs={{0,2},{1,3},{2,0},{3,1},{4,6},{5,7},{6,4},{7,5},{8,10},{9,11},{10,... | collective-permute-start | bytes 786440 | tf_op jit(solution)/shard_map/ppermute | solution.py:25
  13.2 17.1 %collective-permute-start.7 = (bf16[512,256]{1,0:T(8,128)(2,1)S(1)}, bf16[512,256]{1,0:T(8,128)(2,1)S(1)}, u32[]{:S(2)}, u32[]{:S(2)}) collective-permute-start(bf16[512,256]{1,0:T(8,128)(2,1)S(1)} %get-tuple-element.87), channel_id=1, source_target_pairs={{0,2},{1,3},{2,0},{3,1},{4,6},{5,7},{6,4},{7,5},{8,10},{9,11},{10,... | collective-permute-start | bytes 786440 | tf_op jit(solution)/shard_map/ppermute | solution.py:25
  14.6 17.1 %collective-permute-start.2 = (bf16[512,256]{1,0:T(8,128)(2,1)S(1)}, bf16[512,256]{1,0:T(8,128)(2,1)S(1)}, u32[]{:S(2)}, u32[]{:S(2)}) collective-permute-start(bf16[512,256]{1,0:T(8,128)(2,1)S(1)} %collective-permute-done.1.refs_2_), channel_id=1, source_target_pairs={{0,1},{1,0},{2,3},{3,2},{4,5},{5,4},{6,7},{7,6},{8,9},{9,8},{10,11... | collective-permute-start | bytes 786440 | tf_op jit(solution)/shard_map/ppermute | solution.py:25
  19.0 20.6 %collective-permute-start.4 = (bf16[512,256]{1,0:T(8,128)(2,1)S(1)}, bf16[512,256]{1,0:T(8,128)(2,1)S(1)}, u32[]{:S(2)}, u32[]{:S(2)}) collective-permute-start(bf16[512,256]{1,0:T(8,128)(2,1)S(1)} %collective-permute-done.3.refs_2_), channel_id=1, source_target_pairs={{0,1},{1,0},{2,3},{3,2},{4,5},{5,4},{6,7},{7,6},{8,9},{9,8},{10,11... | collective-permute-start | bytes 786440 | tf_op jit(solution)/shard_map/ppermute | solution.py:25
  24.7 20.7 %collective-permute-start.6 = (bf16[512,256]{1,0:T(8,128)(2,1)S(1)}, bf16[512,256]{1,0:T(8,128)(2,1)S(1)}, u32[]{:S(2)}, u32[]{:S(2)}) collective-permute-start(bf16[512,256]{1,0:T(8,128)(2,1)S(1)} %collective-permute-done.5.refs_2_), channel_id=1, source_target_pairs={{0,1},{1,0},{2,3},{3,2},{4,5},{5,4},{6,7},{7,6},{8,9},{9,8},{10,11... | collective-permute-start | bytes 786440 | tf_op jit(solution)/shard_map/ppermute | solution.py:25
  30.3 15.5 %collective-permute-start.8 = (bf16[512,256]{1,0:T(8,128)(2,1)S(1)}, bf16[512,256]{1,0:T(8,128)(2,1)S(1)}, u32[]{:S(2)}, u32[]{:S(2)}) collective-permute-start(bf16[512,256]{1,0:T(8,128)(2,1)S(1)} %collective-permute-done.7.refs_2_), channel_id=1, source_target_pairs={{0,1},{1,0},{2,3},{3,2},{4,5},{5,4},{6,7},{7,6},{8,9},{9,8},{10,11... | collective-permute-start | bytes 786440 | tf_op jit(solution)/shard_map/ppermute | solution.py:25
  36.9 19.7 %collective-permute-start.14 = (bf16[480,256]{1,0:T(8,128)(2,1)}, bf16[480,256]{1,0:T(8,128)(2,1)S(1)}, u32[]{:S(2)}, u32[]{:S(2)}) collective-permute-start(bf16[480,256]{1,0:T(8,128)(2,1)} %get-tuple-element.47.refs_0_), channel_id=1, source_target_pairs={{0,2},{1,3},{2,0},{3,1},{4,6},{5,7},{6,4},{7,5},{8,10},{9,11},{10,... | collective-permute-start | bytes 737288 | tf_op jit(solution)/shard_map/ppermute | solution.py:25
  38.3 18.5 %collective-permute-start.18 = (bf16[480,256]{1,0:T(8,128)(2,1)}, bf16[480,256]{1,0:T(8,128)(2,1)S(1)}, u32[]{:S(2)}, u32[]{:S(2)}) collective-permute-start(bf16[480,256]{1,0:T(8,128)(2,1)} %get-tuple-element.47.refs_0_), channel_id=1, source_target_pairs={{0,1},{1,0},{2,3},{3,2},{4,5},{5,4},{6,7},{7,6},{8,9},{9,8},{10,11... | collective-permute-start | bytes 737288 | tf_op jit(solution)/shard_map/ppermute | solution.py:25
  39.6 12.8 %collective-permute-start.26 = (bf16[256,256]{1,0:T(8,128)(2,1)}, bf16[256,256]{1,0:T(8,128)(2,1)S(1)}, u32[]{:S(2)}, u32[]{:S(2)}) collective-permute-start(bf16[256,256]{1,0:T(8,128)(2,1)} %get-tuple-element.60), channel_id=1, source_target_pairs={{0,34},{1,35},{2,32},{3,33},{4,38},{5,39},{6,36},{7,37},{8,42},{9,... | collective-permute-start | bytes 393224 | tf_op jit(solution)/shard_map/ppermute | solution.py:25
  53.0 15.6 %collective-permute-start.17 = (bf16[544,256]{1,0:T(8,128)(2,1)}, bf16[544,256]{1,0:T(8,128)(2,1)S(1)}, u32[]{:S(2)}, u32[]{:S(2)}) collective-permute-start(bf16[544,256]{1,0:T(8,128)(2,1)} %get-tuple-element.58.refs_3_), channel_id=1, source_target_pairs={{0,2},{1,3},{2,0},{3,1},{4,6},{5,7},{6,4},{7,5},{8,10},{9,11},{10,... | collective-permute-start | bytes 835592 | tf_op jit(solution)/shard_map/ppermute | solution.py:25
  53.7 13.0 %collective-permute-start.16 = (bf16[512,256]{1,0:T(8,128)(2,1)S(1)}, bf16[512,256]{1,0:T(8,128)(2,1)S(1)}, u32[]{:S(2)}, u32[]{:S(2)}) collective-permute-start(bf16[512,256]{1,0:T(8,128)(2,1)S(1)} %copy-done.6), channel_id=1, source_target_pairs={{0,2},{1,3},{2,0},{3,1},{4,6},{5,7},{6,4},{7,5},{8,10},{9,11},{10,... | collective-permute-start | bytes 786440 | tf_op jit(solution)/shard_map/ppermute | solution.py:25
  55.8 12.9 %collective-permute-start.20 = (bf16[512,256]{1,0:T(8,128)(2,1)S(1)}, bf16[512,256]{1,0:T(8,128)(2,1)S(1)}, u32[]{:S(2)}, u32[]{:S(2)}) collective-permute-start(bf16[512,256]{1,0:T(8,128)(2,1)S(1)} %copy-done.6), channel_id=1, source_target_pairs={{0,1},{1,0},{2,3},{3,2},{4,5},{5,4},{6,7},{7,6},{8,9},{9,8},{10,11... | collective-permute-start | bytes 786440 | tf_op jit(solution)/shard_map/ppermute | solution.py:25
  56.6 24.9 %collective-permute-start.15 = (bf16[512,256]{1,0:T(8,128)(2,1)S(1)}, bf16[512,256]{1,0:T(8,128)(2,1)S(1)}, u32[]{:S(2)}, u32[]{:S(2)}) collective-permute-start(bf16[512,256]{1,0:T(8,128)(2,1)S(1)} %copy-done.5), channel_id=1, source_target_pairs={{0,2},{1,3},{2,0},{3,1},{4,6},{5,7},{6,4},{7,5},{8,10},{9,11},{10,... | collective-permute-start | bytes 786440 | tf_op jit(solution)/shard_map/ppermute | solution.py:25
  57.5 24.5 %collective-permute-start.19 = (bf16[512,256]{1,0:T(8,128)(2,1)S(1)}, bf16[512,256]{1,0:T(8,128)(2,1)S(1)}, u32[]{:S(2)}, u32[]{:S(2)}) collective-permute-start(bf16[512,256]{1,0:T(8,128)(2,1)S(1)} %copy-done.5), channel_id=1, source_target_pairs={{0,1},{1,0},{2,3},{3,2},{4,5},{5,4},{6,7},{7,6},{8,9},{9,8},{10,11... | collective-permute-start | bytes 786440 | tf_op jit(solution)/shard_map/ppermute | solution.py:25
  66.8 26.8 %collective-permute-start.21 = (bf16[544,256]{1,0:T(8,128)(2,1)}, bf16[544,256]{1,0:T(8,128)(2,1)S(1)}, u32[]{:S(2)}, u32[]{:S(2)}) collective-permute-start(bf16[544,256]{1,0:T(8,128)(2,1)} %get-tuple-element.58.refs_3_), channel_id=1, source_target_pairs={{0,1},{1,0},{2,3},{3,2},{4,5},{5,4},{6,7},{7,6},{8,9},{9,8},{10,11... | collective-permute-start | bytes 835592 | tf_op jit(solution)/shard_map/ppermute | solution.py:25
  68.6 28.6 %collective-permute-start.25 = (bf16[544,256]{1,0:T(8,128)(2,1)S(1)}, bf16[544,256]{1,0:T(8,128)(2,1)S(1)}, u32[]{:S(2)}, u32[]{:S(2)}) collective-permute-start(bf16[544,256]{1,0:T(8,128)(2,1)S(1)} %collective-permute-done.17.refs_7_), channel_id=1, source_target_pairs={{0,1},{1,0},{2,3},{3,2},{4,5},{5,4},{6,7},{7,6},{8,9},{9,8},{10,11... | collective-permute-start | bytes 835592 | tf_op jit(solution)/shard_map/ppermute | solution.py:25
  68.7 28.0 %collective-permute-start.24 = (bf16[512,256]{1,0:T(8,128)(2,1)S(1)}, bf16[512,256]{1,0:T(8,128)(2,1)S(1)}, u32[]{:S(2)}, u32[]{:S(2)}) collective-permute-start(bf16[512,256]{1,0:T(8,128)(2,1)S(1)} %collective-permute-done.16.refs_6_), channel_id=1, source_target_pairs={{0,1},{1,0},{2,3},{3,2},{4,5},{5,4},{6,7},{7,6},{8,9},{9,8},{10,11... | collective-permute-start | bytes 786440 | tf_op jit(solution)/shard_map/ppermute | solution.py:25
  69.2 24.2 %all-to-all-start = ((f32[64,4,128]{2,1,0:T(4,128)}), f32[64,4,128]{2,1,0:T(4,128)S(1)}, u32[]{:S(2)}, u32[]{:S(2)}) async-start(f32[64,4,128]{2,1,0:T(4,128)} %get-tuple-element.63), calls=%async_computation | async-start | bytes 262144 | tf_op jit(solution)/shard_map/all_to_all | solution.py:353
  81.5 15.8 %collective-permute-start.23 = (bf16[512,256]{1,0:T(8,128)(2,1)S(1)}, bf16[512,256]{1,0:T(8,128)(2,1)S(1)}, u32[]{:S(2)}, u32[]{:S(2)}) collective-permute-start(bf16[512,256]{1,0:T(8,128)(2,1)S(1)} %collective-permute-done.15.refs_5_), channel_id=1, source_target_pairs={{0,1},{1,0},{2,3},{3,2},{4,5},{5,4},{6,7},{7,6},{8,9},{9,8},{10,11... | collective-permute-start | bytes 786440 | tf_op jit(solution)/shard_map/ppermute | solution.py:25
  82.0 12.8 %collective-permute-start.22 = (bf16[480,256]{1,0:T(8,128)(2,1)}, bf16[480,256]{1,0:T(8,128)(2,1)}, u32[]{:S(2)}, u32[]{:S(2)}) collective-permute-start(bf16[480,256]{1,0:T(8,128)(2,1)} %copy-done.8), channel_id=1, source_target_pairs={{0,1},{1,0},{2,3},{3,2},{4,5},{5,4},{6,7},{7,6},{8,9},{9,8},{10,11... | collective-permute-start | bytes 737288 | tf_op jit(solution)/shard_map/ppermute | solution.py:25
  93.6 11.6 %collective-permute-start.29 = (f32[16,128]{1,0:T(8,128)S(1)}, f32[16,128]{1,0:T(8,128)S(1)}, u32[]{:S(2)}, u32[]{:S(2)}) collective-permute-start(f32[16,128]{1,0:T(8,128)S(1)} %combine.1.refs_20_.refs_16_), channel_id=1, source_target_pairs={{0,2},{1,3},{2,0},{3,1},{4,6},{5,7},{6,4},{7,5},{8,10},{9,11},{10,... | collective-permute-start | bytes 24584 | tf_op jit(solution)/shard_map/ppermute | solution.py:25
  94.7 10.4 %collective-permute-start.30 = (f32[16,128]{1,0:T(8,128)S(1)}, f32[16,128]{1,0:T(8,128)S(1)}, u32[]{:S(2)}, u32[]{:S(2)}) collective-permute-start(f32[16,128]{1,0:T(8,128)S(1)} %combine.1.refs_20_.refs_16_), channel_id=1, source_target_pairs={{0,1},{1,0},{2,3},{3,2},{4,5},{5,4},{6,7},{7,6},{8,9},{9,8},{10,11... | collective-permute-start | bytes 24584 | tf_op jit(solution)/shard_map/ppermute | solution.py:25
  (33 other events, 262.2 us)
